TPU v7x, 32 devices: a whole 2x2x4 slice. The times are simulated.
32 devices in a mesh: tm: 8 (over z, x), tensor: 4 (over y, core).
Axes of the slice: x: 2, y: 2, z: 4, core: 2. Of those that a mesh axis runs over, the one named last changes fastest.
Arguments:
- latents: float32 [8, 640, 64], P('tm', 'tensor'), may hold values from -6 to 6
- residual: bfloat16 [8, 640, 5120], P('tm'), may hold values from -6 to 6
- timesteps: int32 [8], P('tm'), may hold values from 0 to 999
- step_sizes: float32 [8], P('tm'), may hold values from 0.015 to 0.06
- embed_weight: bfloat16 [64, 5120], replicated
- mod_weight: bfloat16 [3, 256, 5120], P(None, None, 'tensor'), may hold values from -0.75 to 0.75
- up_weight: bfloat16 [5120, 7168], P('tm', 'tensor'), may hold values from -0.078125 to 0.078125
- down_weight: bfloat16 [7168, 5120], P('tensor', 'tm'), may hold values from -0.0625 to 0.0625
- head_weight: bfloat16 [5120, 64], replicated, may hold values from -0.078125 to 0.078125
Outputs:
- drift: float32 [8, 640, 64], P('tm', 'tensor')
- new_latents: float32 [8, 640, 64], P('tm', 'tensor')
All inputs are finite; a program needn't handle non-finite values.
Results may differ from a plain program's by a relative error of at most 0.0085.
Values may be sent and summed in bfloat16 or wider, within the bound.
A program may use at most 128 MiB of HBM per device.

v0:
```python
import functools
import math

import jax
import jax.numpy as jnp
from jax import lax
from jax.experimental import pallas as pl
from jax.experimental.pallas import tpu as pltpu
from jax.sharding import PartitionSpec as P

MESH = pl.DeviceIdType.MESH
F32 = jnp.float32
BF16 = jnp.bfloat16
LANE = 128
RING = 3


def normalize(values):
    centre = values - jnp.mean(values, axis=-1, keepdims=True)
    spread = jnp.mean(centre * centre, axis=-1, keepdims=True)
    return centre * lax.rsqrt(spread + 1e-06)


def time_features(stamps, width):
    half = width // 2
    freqs = jnp.exp(-math.log(10000.0) * jnp.arange(half, dtype=F32) / half)
    angles = stamps.astype(F32)[:, None] * freqs[None, :]
    return jnp.concatenate([jnp.cos(angles), jnp.sin(angles)], axis=-1)


def bit_of(value, bit):
    return lax.rem(lax.div(value, jnp.int32(1 << bit)), jnp.int32(2))


def flip(value, mask):
    bit = 0
    while (1 << bit) <= mask:
        if mask & (1 << bit):
            value = value + (1 << bit) - (2 << bit) * bit_of(value, bit)
        bit += 1
    return value


def reversed_bits(value, bits):
    total = 0
    for b in range(bits):
        total = total + bit_of(value, b) * (1 << (bits - 1 - b))
    return total


def static_reversed(value, bits):
    return sum(((value >> b) & 1) << (bits - 1 - b) for b in range(bits))


def cut(extent, width=256):
    return [(a, min(width, extent - a)) for a in range(0, extent, width)]


def block_kernel(dims, normed, ups, downs, near, far, *scratch):
    n_tm, n_tensor, own, depth, half = dims
    line, bits = n_tm // 2, n_tensor.bit_length() - 1
    levels = bits + 1
    up_cuts, down_cuts = cut(half), cut(depth)
    (acts, up_all, down_all, part_out, part_in, part_keep, hidden, far_in) = scratch[:8]
    gives = scratch[8 : 8 + levels]
    takes = scratch[8 + levels : 8 + 2 * levels]
    keeps = scratch[8 + 2 * levels : 8 + 3 * levels]
    last_give = scratch[8 + 3 * levels]
    (own_sem, swap_s, swap_r, spread_s, spread_r, up_s, up_r, down_s, down_r,
     part_s, part_r, act_s, act_r, red_s, red_r, far_s, far_r) = scratch[9 + 3 * levels :]

    me, col = lax.axis_index("tm"), lax.axis_index("tensor")
    place, side = lax.div(me, jnp.int32(2)), lax.rem(me, jnp.int32(2))
    zbit = bit_of(place, 0)
    other = 1 - side
    pos = reversed_bits(col, bits)
    core = bit_of(col, 0)
    rows = n_tensor * own
    tile = rows

    def device(tm_mask, tensor_mask=0):
        return {"tm": flip(me, tm_mask), "tensor": flip(col, tensor_mask)}

    def remote(src, dst, send, recv, to):
        return pltpu.make_async_remote_copy(
            src_ref=src, dst_ref=dst, send_sem=send, recv_sem=recv,
            device_id=to, device_id_type=MESH,
        )

    peers = [(2 * k, 0) for k in range(1, line)] + [(1, 0), (3, 0)]
    peers += [(0, 1 << b) for b in range(bits)]
    barrier = pltpu.get_barrier_semaphore()
    for tm_mask, tensor_mask in peers:
        pl.semaphore_signal(
            barrier, inc=1, device_id=device(tm_mask, tensor_mask), device_id_type=MESH
        )
    pl.semaphore_wait(barrier, len(peers))

    pending = []

    def start(copy):
        copy.start()
        pending.append(copy)
        return copy

    mine = pl.ds(pl.multiple_of(col * own, own), own)
    arrivals = []
    for e, (dx, dz) in enumerate(((1, 0), (0, 1), (1, 1))):
        kside = other if dx else side
        start(remote(normed.at[kside, mine], acts.at[side, pos, zbit],
                     swap_s.at[e], swap_r.at[e], device(dx + 2 * dz)))
        sx = other if dx else side
        sz = 1 - zbit if dz else zbit
        arrivals.append((sx, sz))
    local = []
    for j in range(n_tensor):
        copy = pltpu.make_async_copy(
            normed.at[side, pl.ds(j * own, own)],
            acts.at[side, static_reversed(j, bits), zbit], own_sem.at[j])
        copy.start()
        local.append(copy)

    def up_copy(c, k):
        off, width = up_cuts[c]
        want = 1 - zbit if k % 2 else zbit
        src = ups.at[:, pl.ds(pl.multiple_of(want * half + off, LANE), width)]
        dst = up_all.at[place, :, off : off + width]
        if k == 0:
            return pltpu.make_async_copy(src, dst, up_r.at[c, 0])
        return remote(src, dst, up_s.at[c, k], up_r.at[c, k], device(2 * k))

    def up_arrival(c, k):
        off, width = up_cuts[c]
        dst = up_all.at[flip(place, k), :, off : off + width]
        return remote(dst, dst, up_s.at[c, k], up_r.at[c, k], device(2 * k))

    def down_copy(c, k):
        off, width = down_cuts[c]
        want = 1 - zbit if k % 2 else zbit
        src = downs.at[pl.ds(pl.multiple_of(want * half, LANE), half), off : off + width]
        dst = down_all.at[place, :, off : off + width]
        if k == 0:
            return pltpu.make_async_copy(src, dst, down_r.at[c, 0])
        return remote(src, dst, down_s.at[c, k], down_r.at[c, k], device(2 * k))

    def send_downs(m, c):
        for k in (2 * m, 2 * m + 1):
            copy = down_copy(c, k)
            if k == 0:
                copy.start()
            else:
                start(copy)

    for c in range(len(up_cuts)):
        for k in range(line):
            copy = up_copy(c, k)
            if k == 0:
                copy.start()
            else:
                start(copy)
    groups = [(m, c) for m in range(line // 2) for c in range(len(down_cuts))]
    early = len(groups) * 2 // 3
    for m, c in groups[:early]:
        send_downs(m, c)

    def spread(e, s):
        sx, sz = arrivals[e]
        count = 1 << s
        first = pos - lax.rem(pos, jnp.int32(count))
        block = acts.at[sx, pl.ds(first, count), sz]
        return remote(block, block, spread_s.at[e, s], spread_r.at[e, s],
                      device(0, n_tensor >> (s + 1)))

    def spread_arrival(e, s):
        sx, sz = arrivals[e]
        count = 1 << s
        first = flip(pos - lax.rem(pos, jnp.int32(count)), count)
        block = acts.at[sx, pl.ds(first, count), sz]
        return remote(block, block, spread_s.at[e, s], spread_r.at[e, s],
                      device(0, n_tensor >> (s + 1)))

    for e, (sx, sz) in enumerate(arrivals):
        block = acts.at[sx, pos, sz]
        remote(block, block, swap_s.at[e], swap_r.at[e], device(1)).wait_recv()
        start(spread(e, 0))
    for s in range(1, bits):
        for e in range(3):
            spread_arrival(e, s - 1).wait_recv()
            start(spread(e, s))
    for e in range(3):
        spread_arrival(e, bits - 1).wait_recv()
    for copy in local:
        copy.wait()

    hp = n_tensor // 2
    kdim = line * depth

    def rows_of(which, h):
        return acts[which, pl.ds(h * hp, hp)].reshape(tile, kdim)

    def part_copy(c):
        off, width = up_cuts[c]
        return remote(part_out.at[:, :, off : off + width], part_in.at[:, :, off : off + width],
                      part_s.at[c], part_r.at[c], device(1))

    def act_copy(c, which):
        off, width = up_cuts[c]
        block = hidden.at[which, :, :, off : off + width]
        return remote(block, block, act_s.at[c], act_r.at[c], device(1))

    def first_product(c):
        off, width = up_cuts[c]
        up_copy(c, 0).wait()
        for k in range(1, line):
            up_arrival(c, k).wait_recv()

        def give(h, carry):
            weight = up_all[:, :, off : off + width].reshape(kdim, width)
            out = jnp.dot(rows_of(other, h), weight, preferred_element_type=F32)
            part_out[h, :, off : off + width] = out.astype(BF16)
            return carry

        def keep(h, carry):
            weight = up_all[:, :, off : off + width].reshape(kdim, width)
            out = jnp.dot(rows_of(side, h), weight, preferred_element_type=F32)
            part_keep[c % 2, h, :, :width] = out
            return carry

        lax.fori_loop(0, 2, give, 0)
        start(part_copy(c))
        lax.fori_loop(0, 2, keep, 0)

    def activate(c):
        off, width = up_cuts[c]
        part_copy(c).wait_recv()

        def body(h, carry):
            total = part_keep[c % 2, h, :, :width] + part_in[h, :, off : off + width].astype(F32)
            hidden[side, h, :, off : off + width] = jax.nn.gelu(total, approximate=True).astype(BF16)
            return carry

        lax.fori_loop(0, 2, body, 0)
        start(act_copy(c, side))

    for c in range(len(up_cuts)):
        first_product(c)
        if c > 0:
            activate(c - 1)
    activate(len(up_cuts) - 1)
    for m, c in groups[early:]:
        send_downs(m, c)
    for c in range(len(up_cuts)):
        act_copy(c, other).wait_recv()

    order = [(2 * m + p, c) for m, c in groups for p in range(2)]
    base = place - zbit
    split_bits = [bit_of(col, b) for b in range(1, bits)] + [zbit]
    masks = [(0, 1 << b) for b in range(bits)] + [(2, 0)]
    sizes = [rows >> b for b in range(levels)]

    def slab_of(p):
        return flip(base, p - p % 2) + p % 2

    def level_copy(level, t):
        p, c = order[t]
        off, width = down_cuts[c]
        return remote(gives[level].at[t % RING, :, :, :width],
                      takes[level].at[slab_of(p), :, :, off : off + width],
                      red_s.at[level, t], red_r.at[level, t], device(*masks[level]))

    def far_copy(t):
        p, c = order[t]
        off, width = down_cuts[c]
        return remote(last_give.at[t % RING, :, :width],
                      far_in.at[slab_of(p), :, off : off + width],
                      far_s.at[t], far_r.at[t], device(1))

    def second_product(t):
        p, c = order[t]
        off, width = down_cuts[c]
        slab = slab_of(p)
        wait_slab(p, c)
        if t >= RING:
            level_copy(0, t - RING).wait_send()

        def give(x, carry):
            out = jnp.dot(hidden[x, 1 - core], down_all[slab, :, off : off + width],
                          preferred_element_type=F32)
            gives[0][t % RING, x, :, :width] = out.astype(BF16)
            return carry

        def keep(x, carry):
            out = jnp.dot(hidden[x, core], down_all[slab, :, off : off + width],
                          preferred_element_type=F32)
            keeps[0][t % 2, x, :, :width] = out.astype(BF16)
            return carry

        lax.fori_loop(0, 2, give, 0)
        level_copy(0, t).start()
        lax.fori_loop(0, 2, keep, 0)

    def wait_slab(p, c):
        off, width = down_cuts[c]
        dst = down_all.at[slab_of(p), :, off : off + width]
        pltpu.make_async_copy(dst, dst, down_r.at[c, slab_index(p)]).wait()

    def slab_index(p):
        return p + zbit * (1 - 2 * (p % 2))

    def reduce_level(level, t):
        p, c = order[t]
        off, width = down_cuts[c]
        slab = slab_of(p)
        level_copy(level, t).wait_recv()
        size = sizes[level]
        last = level == levels - 1

        def total(x, first, count):
            taken = takes[level][slab, x, pl.ds(first, count), off : off + width].astype(F32)
            return keeps[level][t % 2, x, pl.ds(first, count), :width].astype(F32) + taken

        if last:
            if t >= RING:
                far_copy(t - RING).wait_send()
            last_give[t % RING, :, :width] = total(other, 0, size).astype(BF16)
            far_copy(t).start()
            near[slab, :, off : off + width] = total(side, 0, size)
            return
        if t >= RING:
            level_copy(level + 1, t - RING).wait_send()
        count = size // 2
        bit = split_bits[level]
        away = pl.multiple_of((1 - bit) * count, 16)
        here = pl.multiple_of(bit * count, 16)
        for x in range(2):
            gives[level + 1][t % RING, x, :, :width] = total(x, away, count).astype(BF16)
        level_copy(level + 1, t).start()
        for x in range(2):
            keeps[level + 1][t % 2, x, :, :width] = total(x, here, count)

    count = len(order)
    for i in range(count + levels):
        if i < count:
            second_product(i)
        for level in range(levels):
            t = i - 1 - level
            if 0 <= t < count:
                reduce_level(level, t)
    for t in range(count):
        far_copy(t).wait_recv()
    far[...] = far_in[...]

    for copy in pending:
        copy.wait_send()
    for t in range(max(count - RING, 0), count):
        for level in range(levels):
            level_copy(level, t).wait_send()
        far_copy(t).wait_send()


def feed_forward(normed, ups, downs, n_tm, n_tensor, own):
    line, bits = n_tm // 2, n_tensor.bit_length() - 1
    levels = bits + 1
    depth, half = ups.shape[0], downs.shape[0] // 2
    rows = n_tensor * own
    up_n, down_n = len(cut(half)), len(cut(depth))
    chunks = down_n * line
    wide = min(256, depth)
    sizes = [rows >> b for b in range(levels)]
    scratch = [
        pltpu.VMEM((2, n_tensor, 2, own, line * depth), BF16),
        pltpu.VMEM((line, depth, half), BF16),
        pltpu.VMEM((line, half, depth), BF16),
        pltpu.VMEM((2, rows, half), BF16),
        pltpu.VMEM((2, rows, half), BF16),
        pltpu.VMEM((2, 2, rows, min(256, half)), F32),
        pltpu.VMEM((2, 2, rows, half), BF16),
        pltpu.VMEM((line, own, depth), BF16),
    ]
    scratch += [pltpu.VMEM((RING, 2, size, wide), BF16) for size in sizes]
    scratch += [pltpu.VMEM((line, 2, size, depth), BF16) for size in sizes]
    scratch += [
        pltpu.VMEM((2, 2, size, wide), BF16 if level == 0 else F32)
        for level, size in enumerate(sizes)
    ]
    scratch += [pltpu.VMEM((RING, own, wide), BF16)]
    dma = pltpu.SemaphoreType.DMA
    scratch += [
        dma((n_tensor,)), dma((3,)), dma((3,)), dma((3, bits)), dma((3, bits)),
        dma((up_n, line)), dma((up_n, line)), dma((down_n, line)), dma((down_n, line)),
        dma((up_n,)), dma((up_n,)), dma((up_n,)), dma((up_n,)),
        dma((levels, chunks)), dma((levels, chunks)), dma((chunks,)), dma((chunks,)),
    ]
    return pl.pallas_call(
        functools.partial(block_kernel, (n_tm, n_tensor, own, depth, half)),
        out_shape=(
            jax.ShapeDtypeStruct((line, own, depth), F32),
            jax.ShapeDtypeStruct((line, own, depth), BF16),
        ),
        in_specs=[pl.BlockSpec(memory_space=pl.ANY)] * 3,
        out_specs=(pl.BlockSpec(memory_space=pltpu.VMEM),) * 2,
        scratch_shapes=scratch,
        compiler_params=pltpu.CompilerParams(
            collective_id=0, has_side_effects=True, vmem_limit_bytes=67043328
        ),
    )(normed, ups, downs)


def make_local(n_tm, n_tensor):
    line = n_tm // 2
    swap = [(i, i ^ 1) for i in range(n_tm)]

    def local(
        latents,
        residual,
        timesteps,
        step_sizes,
        embed_weight,
        mod_weight,
        up_weight,
        down_weight,
        head_weight,
    ):
        position = lax.axis_index("tm")
        column = lax.axis_index("tensor")
        side = position % 2
        latent = latents[0]
        stream = residual[0]
        tokens, width = stream.shape
        own_rows = latent.shape[0]
        depth = up_weight.shape[0]
        half = up_weight.shape[1] // 2
        pad_d, pad_h = -depth % LANE, -half % LANE

        feature = jax.nn.silu(time_features(timesteps, mod_weight.shape[1])).astype(BF16)[0]
        piece_mod = jnp.einsum("f,kfd->kd", feature, mod_weight, preferred_element_type=F32)
        modulation = lax.all_gather(piece_mod, "tensor", axis=1, tiled=True)
        latent_bf = latent.astype(BF16)
        every_latent = lax.all_gather(latent_bf, "tensor", axis=0, tiled=True)

        def modulate(values):
            return (normalize(values) * (1.0 + modulation[1]) + modulation[0]).astype(BF16)

        row_start = column * own_rows
        hidden = lax.dynamic_slice_in_dim(stream, row_start, own_rows, 0).astype(F32) + jnp.dot(
            latent_bf, embed_weight, preferred_element_type=F32
        )
        every_hidden = stream.astype(F32) + jnp.dot(
            every_latent, embed_weight, preferred_element_type=F32
        )
        normed = modulate(every_hidden)
        sides = []
        for s in range(2):
            slabs = []
            for k in range(line):
                slab = normed[:, (2 * k + s) * depth : (2 * k + s + 1) * depth]
                slabs.append(jnp.pad(slab, ((0, 0), (0, pad_d))) if pad_d else slab)
            sides.append(jnp.concatenate(slabs, axis=1))
        normed = jnp.stack(sides)
        ups, downs = up_weight, down_weight
        if pad_d or pad_h:
            ups = jnp.pad(ups.reshape(depth, 2, half), ((0, pad_d), (0, 0), (0, pad_h)))
            ups = ups.reshape(depth + pad_d, -1)
            downs = jnp.pad(downs.reshape(2, half, depth), ((0, 0), (0, pad_h), (0, pad_d)))
            downs = downs.reshape(-1, depth + pad_d)
        near, far = feed_forward(normed, ups, downs, n_tm, n_tensor, own_rows)
        near, far = near[:, :, :depth], far[:, :, :depth].astype(F32)
        pieces = []
        for k in range(line):
            pieces.append(jnp.where(side == 0, near[k], far[k]))
            pieces.append(jnp.where(side == 0, far[k], near[k]))
        mixed = jnp.concatenate(pieces, axis=-1)

        updated = hidden + modulation[2] * mixed
        drift = jnp.dot(
            normalize(updated).astype(BF16), head_weight, preferred_element_type=F32
        )
        first = (position == 0).astype(F32)
        term = first * latent - step_sizes[0] * drift
        beside = lax.ppermute(term, "tm", swap)
        couple = term + beside
        new_latent = term + jnp.where(side == 1, beside, 0.0)
        for k in range(1, line):
            ahead = [(i, i + 2 * k) for i in range(n_tm - 2 * k)]
            new_latent = new_latent + lax.ppermute(couple, "tm", ahead)
        return (drift[None], new_latent[None])

    return local


def solution(mesh):
    in_specs = (
        P("tm", "tensor", None),
        P("tm", None, None),
        P("tm"),
        P("tm"),
        P(),
        P(None, None, "tensor"),
        P("tm", "tensor"),
        P("tensor", "tm"),
        P(),
    )
    out_specs = (P("tm", "tensor", None), P("tm", "tensor", None))
    local = make_local(mesh.shape["tm"], mesh.shape["tensor"])
    return jax.shard_map(local, mesh=mesh, in_specs=in_specs, out_specs=out_specs, check_vma=False)
```

profile of v0, /device:TPU:0, one launch (start us, length us, event | category | flops | bytes accessed | tf_op | source)
XLA Modules:
  0.0 361.5 jit_solution(3197740921224589753)
XLA Ops:
  0.6 0.8 convert_element_type.41
  1.5 0.6 copy-done.3
  2.2 7.6 %all-gather = bf16[1,640,64]{2,0,1:T(2,128)(2,1)S(1)} all-gather(bf16[1,160,64]{2,0,1:T(2,128)(2,1)S(1)} %copy.12), channel_id=2, replica_groups=mesh['tm'=8,'tensor'=4] {'tensor'}, dimensions={1}, use_global_device_ids=true | all-gather | bytes 102400 | tf_op jit(solution)/shard_map/all_gather | solution.py:439
  10.0 5.1 %fusion.11 = (f32[640]{0:T(1024)S(1)}, f32[640,5120]{1,0:T(8,128)S(1)}) fusion(bf16[64,5120]{1,0:T(8,128)(2,1)} %param.13, bf16[1,640,64]{1,2,0:T(8,128)(2,1)S(1)} %copy.13, bf16[1,640,5120]{2,1,0:T(8,128)(2,1)} %param.10), kind=kOutput, calls=%fused_computation.39 | convolution fusion | flops 429260160 | bytes 20400640 | tf_op jit(solution)/shard_map/dot_general | solution.py:448
  15.1 1.4 multiply_reduce_fusion
  16.5 3.6 copy-done
  21.2 5.3 %all_gather.6 = f32[3,5120]{1,0:T(4,128)S(1)} all-gather(f32[3,1280]{1,0:T(4,128)S(1)} %bitcast.58), channel_id=1, replica_groups=mesh['tm'=8,'tensor'=4] {'tensor'}, dimensions={1}, use_global_device_ids=true | all-gather | bytes 76800 | tf_op jit(solution)/shard_map/all_gather | solution.py:437
  26.5 0.7 fusion.10
  27.2 10.5 %add_convert_fusion = bf16[640,5120]{1,0:T(8,128)(2,1)} fusion(f32[640,5120]{1,0:T(8,128)} %copy-done, f32[5120]{0:T(1024)S(1)} %bitcast.56, f32[5120]{0:T(1024)S(1)} %bitcast.57, f32[640]{0:T(1024)S(1)} %add_rsqrt_fusion, f32[640]{0:T(1024)S(1)} %broadcast_multiply_fusion), kind=kLoop, calls=%fused_computation.1 | loop fusion | flops 16384000 | bytes 19706880 | tf_op jit(solution)/shard_map/convert_element_type | solution.py:442
  37.7 3.6 %fusion.9 = (bf16[640,640]{1,0:T(8,128)(2,1)S(1)}, bf16[640,640]{1,0:T(8,128)(2,1)S(1)}, bf16[640,640]{1,0:T(8,128)(2,1)S(1)}, bf16[640,640]{1,0:T(8,128)(2,1)S(...) fusion(bf16[640,5120]{1,0:T(8,128)(2,1)} %add_convert_fusion), kind=kLoop, calls=%fused_computation.37 | loop fusion | bytes 13107200 | tf_op jit(solution)/shard_map/slice | solution.py:456
  41.3 0.5 maximum_bitcast_fusion
  42.1 3.3 pad_maximum_fusion.normed
  45.4 284.3 %shard_map.104 = (f32[4,160,640]{2,1,0:T(8,128)}, bf16[4,160,640]{2,1,0:T(8,128)(2,1)}) custom-call(bf16[2,640,2560]{2,1,0:T(8,128)(2,1)} %pad_maximum_fusion.normed, bf16[640,1792]{1,0:T(8,128)(2,1)} %ups.1, bf16[1792,640]{1,0:T(8,128)(2,1)} %downs.1), custom_call_target="tpu_custom_call" | custom-call | tf_op jit(solution)/shard_map/pallas_call | solution.py:394
  329.7 1.4 convert_element_type.48
  331.1 1.8 bitcast_dynamic-update-slice_fusion.7
  332.9 0.8 bitcast_dynamic-update-slice_fusion.6
  333.8 0.8 bitcast_dynamic-update-slice_fusion.5
  334.6 0.8 bitcast_dynamic-update-slice_fusion.4
  335.4 0.8 bitcast_dynamic-update-slice_fusion.3
  336.3 0.9 bitcast_dynamic-update-slice_fusion.2
  337.1 0.8 bitcast_dynamic-update-slice_fusion.1
  337.9 0.8 bitcast_dynamic-update-slice_fusion
  338.8 3.5 fusion.12
  343.5 2.5 bitcast_subtract_fusion
  345.9 2.2 collective-permute-start
  348.1 2.2 collective-permute-done
  350.4 3.3 collective-permute-start.1
  353.7 4.0 %collective-permute-start.2 = (f32[160,64]{0,1:T(8,128)S(1)}, f32[160,64]{0,1:T(8,128)S(1)}, u32[]{:S(2)}, u32[]{:S(2)}) collective-permute-start(f32[160,64]{0,1:T(8,128)S(1)} %add.93), channel_id=1, source_target_pairs={{0,16},{4,20},{8,24},{12,28},{1,17},{5,21},{9,25},{13,29},{2,18},{... | collective-permute-start | bytes 122888 | tf_op jit(solution)/shard_map/ppermute | solution.py:485
  357.7 1.3 collective-permute-start.3
  359.0 0.6 collective-permute-done.2
  359.6 1.3 collective-permute-done.3
  360.9 0.7 add_bitcast_fusion
  (27 shorter events, 1.5 us)
Async XLA Ops:
  1.5 0.6 copy-start.3
  15.0 5.1 %copy-start = (f32[640,5120]{1,0:T(8,128)}, f32[640,5120]{1,0:T(8,128)S(1)}, u32[]{:S(2)}) copy-start(f32[640,5120]{1,0:T(8,128)S(1)} %get-tuple-element.18) | copy-start | bytes 39321604
  15.1 5.8 %copy-start.2 = (bf16[3,256,1280]{2,1,0:T(8,128)(2,1)S(1)}, bf16[3,256,1280]{2,1,0:T(8,128)(2,1)}, u32[]{:S(2)}) copy-start(bf16[3,256,1280]{2,1,0:T(8,128)(2,1)} %param.14) | copy-start | bytes 5898244
  329.7 3.2 copy-start.1
  334.6 4.2 %copy-start.4 = (bf16[1,160,64]{1,2,0:T(8,128)(2,1)S(1)}, bf16[1,160,64]{1,2,0:T(8,128)(2,1)}, u32[]{:S(2)}) copy-start(bf16[1,160,64]{1,2,0:T(8,128)(2,1)} %copy-done.3) | copy-start | bytes 61444
  334.6 4.2 %copy-start.6 = (f32[1,5120]{1,0:T(1,128)S(1)}, f32[1,5120]{1,0:T(1,128)}, u32[]{:S(2)}) copy-start(f32[1,5120]{1,0:T(1,128)} %get-tuple-element.14) | copy-start | bytes 61444
  342.3 1.2 copy-start.5
  345.9 4.4 %collective-permute-start = (f32[160,64]{0,1:T(8,128)S(1)}, f32[160,64]{0,1:T(8,128)S(1)}, u32[]{:S(2)}, u32[]{:S(2)}) collective-permute-start(f32[160,64]{0,1:T(8,128)S(1)} %get-tuple-element.21), channel_id=1, source_target_pairs={{0,4},{4,0},{8,12},{12,8},{16,20},{20,16},{24,28},{28,24},{1,5},{5... | collective-permute-start | bytes 122888 | tf_op jit(solution)/shard_map/ppermute | solution.py:480
  350.4 8.6 %collective-permute-start.1 = (f32[160,64]{0,1:T(8,128)S(1)}, f32[160,64]{0,1:T(8,128)S(1)}, u32[]{:S(2)}, u32[]{:S(2)}) collective-permute-start(f32[160,64]{0,1:T(8,128)S(1)} %add.93), channel_id=1, source_target_pairs={{0,8},{4,12},{8,16},{12,20},{16,24},{20,28},{1,9},{5,13},{9,17},{1... | collective-permute-start | bytes 122888 | tf_op jit(solution)/shard_map/ppermute | solution.py:485
  353.7 5.9 %collective-permute-start.2 = (f32[160,64]{0,1:T(8,128)S(1)}, f32[160,64]{0,1:T(8,128)S(1)}, u32[]{:S(2)}, u32[]{:S(2)}) collective-permute-start(f32[160,64]{0,1:T(8,128)S(1)} %add.93), channel_id=1, source_target_pairs={{0,16},{4,20},{8,24},{12,28},{1,17},{5,21},{9,25},{13,29},{2,18},{... | collective-permute-start | bytes 122888 | tf_op jit(solution)/shard_map/ppermute | solution.py:485
  357.7 3.2 collective-permute-start.3
where the time goes:
time: 362 us
  Pallas kernels  284 us (78%)
  other arithmetic  27.7 us (8%)
  blocking collectives  12.9 us (4%)
  matrix products  11.4 us (3%)
  starting transfers between devices  10.8 us (3%)
  local copies, waits for them, and re-layouts  8.15 us (2%)
  waiting for transfers between devices  4.11 us (1%)
    pallas_call x1, Pallas kernels, feed_forward(): pl.pallas_call(functools.partial(block_kernel, (n_tm, n_tensor, own, dept...  284 us
    convert_element_type x1, other arithmetic, modulate(): (normalize(values) * (1.0 + modulation[1]) + modulation[0]).astype(BF16)  10.5 us
    ppermute x3, starting transfers between devices, local(): new_latent = new_latent + lax.ppermute(couple, 'tm', ahead)  8.62 us
    all_gather x1, blocking collectives, local(): every_latent = lax.all_gather(latent_bf, 'tensor', axis=0, tiled=True)  7.61 us
  transfers between devices with their start and end apart: 4, of which 3 were waited for; matrix products, arithmetic and copies ran while one was open for 0% of the time, Pallas kernels for 0%

commit v1 on v0

v1 whole, which is shorter than its diff:
```python
import functools
import math

import jax
import jax.numpy as jnp
from jax import lax
from jax.experimental import pallas as pl
from jax.experimental.pallas import tpu as pltpu
from jax.sharding import PartitionSpec as P

MESH = pl.DeviceIdType.MESH
F32 = jnp.float32
BF16 = jnp.bfloat16
LANE = 128
GIVE_RING = 3
TAKE_RING = 4
ACT_AT = 2


def time_features(stamps, width):
    half = width // 2
    freqs = jnp.exp(-math.log(10000.0) * jnp.arange(half, dtype=F32) / half)
    angles = stamps.astype(F32)[:, None] * freqs[None, :]
    return jnp.concatenate([jnp.cos(angles), jnp.sin(angles)], axis=-1)


def bit_of(value, bit):
    return lax.rem(lax.div(value, jnp.int32(1 << bit)), jnp.int32(2))


def flip(value, mask):
    bit = 0
    while (1 << bit) <= mask:
        if mask & (1 << bit):
            value = value + (1 << bit) - (2 << bit) * bit_of(value, bit)
        bit += 1
    return value


def reversed_bits(value, bits):
    total = 0
    for b in range(bits):
        total = total + bit_of(value, b) * (1 << (bits - 1 - b))
    return total


def static_reversed(value, bits):
    return sum(((value >> b) & 1) << (bits - 1 - b) for b in range(bits))


def cut(extent, width=256):
    return [(a, min(width, extent - a)) for a in range(0, extent, width)]


def block_kernel(dims, latents, residual, features, sizes, embed, mods, ups, downs, head,
                 drift_out, new_out, *scratch):
    n_tm, n_tensor, own, true_depth, depth, half, subs = dims
    line, bits = n_tm // 2, n_tensor.bit_length() - 1
    levels = bits
    extents = [(n_tensor * own // 2) >> b for b in range(levels)]
    up_cuts, down_cuts = cut(half), cut(depth)
    (acts, up_all, down_all, part_out, part_in, part_keep, hidden, far_in, last_give,
     rows_in, lat_all, mod_in, mod_all, stream, normed, terms, couples,
     far_keep, pair_give, pair_take) = scratch[:20]
    gives = scratch[20 : 20 + levels]
    takes = scratch[20 + levels : 20 + 2 * levels]
    keeps = scratch[20 + 2 * levels : 20 + 3 * levels]
    (row_sem, mod_sem, lat_s, lat_r, modu_s, modu_r, swap_s, swap_r, spread_s, spread_r,
     up_s, up_r, down_s, down_r, part_s, part_r, act_s, act_r, red_s, red_r, pair_s, pair_r,
     far_s, far_r, sum_s, sum_r) = scratch[20 + 3 * levels :]

    me, col = lax.axis_index("tm"), lax.axis_index("tensor")
    place, side = lax.div(me, jnp.int32(2)), lax.rem(me, jnp.int32(2))
    zbit = bit_of(place, 0)
    other = 1 - side
    pos = reversed_bits(col, bits)
    core = bit_of(col, 0)
    rows = n_tensor * own
    hp = n_tensor // 2
    kdim = line * depth
    slabs = n_tm // n_tensor
    features_total = n_tm * true_depth
    chunk_rows = own // subs
    tile = 32 if chunk_rows % 32 == 0 else 16

    def device(tm_mask, tensor_mask=0):
        return {"tm": flip(me, tm_mask), "tensor": flip(col, tensor_mask)}

    def remote(src, dst, send, recv, to):
        return pltpu.make_async_remote_copy(
            src_ref=src, dst_ref=dst, send_sem=send, recv_sem=recv,
            device_id=to, device_id_type=MESH,
        )

    peers = [(2 * k, 0) for k in range(1, line)] + [(1, 0), (3, 0)]
    peers += [(0, f) for f in range(1, n_tensor)]
    barrier = pltpu.get_barrier_semaphore()
    for tm_mask, tensor_mask in peers:
        pl.semaphore_signal(
            barrier, inc=1, device_id=device(tm_mask, tensor_mask), device_id_type=MESH
        )

    def row_copy(f):
        first = pl.multiple_of(flip(col, f) * own, 16)
        return pltpu.make_async_copy(
            residual.at[pl.ds(first, own)], rows_in.at[f % 2], row_sem.at[f])

    mod_copy = pltpu.make_async_copy(mods, mod_in, mod_sem)
    mod_copy.start()
    row_copy(0).start()
    row_copy(1).start()
    lat_all[col] = latents[...].astype(BF16)
    pl.semaphore_wait(barrier, len(peers))

    pending = []

    def start(copy):
        copy.start()
        pending.append(copy)
        return copy

    def up_copy(c, k):
        off, width = up_cuts[c]
        want = 1 - zbit if k % 2 else zbit
        src = ups.at[:, pl.ds(pl.multiple_of(want * half + off, LANE), width)]
        dst = up_all.at[place, :, off : off + width]
        if k == 0:
            return pltpu.make_async_copy(src, dst, up_r.at[c, 0])
        return remote(src, dst, up_s.at[c, k], up_r.at[c, k], device(2 * k))

    def up_arrival(c, k):
        off, width = up_cuts[c]
        dst = up_all.at[flip(place, k), :, off : off + width]
        return remote(dst, dst, up_s.at[c, k], up_r.at[c, k], device(2 * k))

    def send_ups(c):
        for k in range(line):
            copy = up_copy(c, k)
            if k == 0:
                copy.start()
            else:
                start(copy)

    def down_copy(c, k):
        off, width = down_cuts[c]
        want = 1 - zbit if k % 2 else zbit
        src = downs.at[pl.ds(pl.multiple_of(want * half, LANE), half), off : off + width]
        dst = down_all.at[place, :, off : off + width]
        if k == 0:
            return pltpu.make_async_copy(src, dst, down_r.at[c, 0])
        return remote(src, dst, down_s.at[c, k], down_r.at[c, k], device(2 * k))

    def send_downs(m, c):
        for k in (2 * m, 2 * m + 1):
            copy = down_copy(c, k)
            if k == 0:
                copy.start()
            else:
                start(copy)

    send_ups(0)

    def lat_copy(f, block):
        return remote(lat_all.at[block], lat_all.at[block], lat_s.at[f], lat_r.at[f], device(0, f))

    def modu_copy(f, block):
        part = mod_all.at[pl.ds(block * slabs, slabs)]
        return remote(part, part, modu_s.at[f], modu_r.at[f], device(0, f))

    for f in range(1, n_tensor):
        start(lat_copy(f, col))
    mod_copy.wait()
    feature = features[...]
    for i in range(slabs):
        for j in range(3):
            mod_all[col * slabs + i, j : j + 1, :] = jnp.dot(
                feature, mod_in[j, :, i * depth : (i + 1) * depth], preferred_element_type=F32)
    for f in range(1, n_tensor):
        start(modu_copy(f, col))
    row_copy(0).wait()
    for f in range(1, n_tensor):
        modu_copy(f, flip(col, f)).wait_recv()

    def moments(values):
        total = values[0]
        for v in values[1:]:
            total = total + v
        mean = jnp.sum(total, axis=-1, keepdims=True) * (1.0 / features_total)
        centred = [v - mean for v in values]
        if depth != true_depth:
            valid = lax.broadcasted_iota(jnp.int32, centred[0].shape, 1) < true_depth
            centred = [jnp.where(valid, v, 0.0) for v in centred]
        total = centred[0] * centred[0]
        for v in centred[1:]:
            total = total + v * v
        spread = jnp.sum(total, axis=-1, keepdims=True) * (1.0 / features_total)
        return centred, lax.rsqrt(spread + 1e-06)

    def hidden_slabs(slot, block, where):
        lat = lat_all[block, where, :]
        found = []
        for s in range(n_tm):
            cols = slice(s * depth, (s + 1) * depth)
            found.append(rows_in[slot, where, cols].astype(F32)
                         + jnp.dot(lat, embed[:, cols], preferred_element_type=F32))
        return found

    def own_rows(r, carry):
        where = pl.ds(pl.multiple_of(r * tile, tile), tile)
        found = hidden_slabs(0, col, where)
        for s in range(n_tm):
            stream[s, where, :] = found[s]
        centred, scale = moments(found)
        outs = [
            (centred[s] * scale * (1.0 + mod_all[s, 1:2, :]) + mod_all[s, 0:1, :]).astype(BF16)
            for s in range(n_tm)
        ]
        for s in range(n_tm):
            normed[s % 2, where, (s // 2) * depth : (s // 2 + 1) * depth] = outs[s]
        for k in range(line):
            acts[side, pos, zbit, where, k * depth : (k + 1) * depth] = jnp.where(
                side == 0, outs[2 * k], outs[2 * k + 1])
        return carry

    moves = ((1, 0), (0, 1), (1, 1))
    arrivals = [(other if dx else side, 1 - zbit if dz else zbit) for dx, dz in moves]

    def sub_rows(b):
        return pl.ds(b * chunk_rows, chunk_rows)

    def swap_copy(e, b):
        dx, dz = moves[e]
        return remote(normed.at[other if dx else side, sub_rows(b)],
                      acts.at[side, pos, zbit, sub_rows(b)],
                      swap_s.at[e, b], swap_r.at[e, b], device(dx + 2 * dz))

    def swap_arrival(e, b):
        sx, sz = arrivals[e]
        block = acts.at[sx, pos, sz, sub_rows(b)]
        return remote(block, block, swap_s.at[e, b], swap_r.at[e, b], device(1))

    for b in range(subs):
        lax.fori_loop(b * (chunk_rows // tile), (b + 1) * (chunk_rows // tile), own_rows, 0)
        for e in range(3):
            start(swap_copy(e, b))
    groups = [(m, c) for m in range(line // 2) for c in range(len(down_cuts))]
    early = len(groups) * 2 // 3

    for f in range(1, n_tensor):
        block = flip(col, f)
        where_pos = reversed_bits(block, bits)
        if f + 1 < n_tensor:
            row_copy(f + 1).start()
        row_copy(f).wait()
        lat_copy(f, block).wait_recv()

        def other_rows(r, carry):
            where = pl.ds(pl.multiple_of(r * tile, tile), tile)
            centred, scale = moments(hidden_slabs(f % 2, block, where))
            for k in range(line):
                value = jnp.where(side == 0, centred[2 * k], centred[2 * k + 1])
                value = value * scale * (1.0 + mod_all[2 * k + side, 1:2, :])
                value = value + mod_all[2 * k + side, 0:1, :]
                acts[side, where_pos, zbit, where, k * depth : (k + 1) * depth] = value.astype(BF16)
            return carry

        lax.fori_loop(0, own // tile, other_rows, 0)

    def spread_block(e, s, b, far_side):
        sx, sz = arrivals[e]
        count = 1 << s
        first = pos - lax.rem(pos, jnp.int32(count))
        if far_side:
            first = flip(first, count)
        block = acts.at[sx, pl.ds(first, count), sz, sub_rows(b)]
        return remote(block, block, spread_s.at[e, s, b], spread_r.at[e, s, b],
                      device(0, n_tensor >> (s + 1)))

    def advance(e, s, b):
        if s == 0:
            swap_arrival(e, b).wait_recv()
        else:
            spread_block(e, s - 1, b, True).wait_recv()
        if s < bits:
            start(spread_block(e, s, b, False))

    def part_copy(c, d):
        off, width = up_cuts[c]
        return remote(part_out.at[d, :, off : off + width], part_in.at[d, :, off : off + width],
                      part_s.at[c, d], part_r.at[c, d], device(1))

    def act_copy(c, d, which):
        off, width = up_cuts[c]
        block = hidden.at[which, :, zbit if d == 0 else 1 - zbit, :, off : off + width]
        return remote(block, block, act_s.at[c, d], act_r.at[c, d], device(1))

    def first_product(u):
        c, d = units[u]
        off, width = up_cuts[c]
        level = zbit if d == 0 else 1 - zbit
        if c not in arrived:
            arrived.add(c)
            up_copy(c, 0).wait()
            for k in range(1, line):
                up_arrival(c, k).wait_recv()

        def product(which, h):
            weight = up_all[:, :, off : off + width].reshape(kdim, width)
            left = acts[which, pl.ds(h * hp, hp), level].reshape(hp * own, kdim)
            return jnp.dot(left, weight, preferred_element_type=F32)

        def give(h, carry):
            where = pl.ds(pl.multiple_of(h * hp * own, 16), hp * own)
            part_out[d, where, off : off + width] = product(other, h).astype(BF16)
            return carry

        def keep(h, carry):
            where = pl.ds(pl.multiple_of(h * hp * own, 16), hp * own)
            part_keep[u % 2, where, :width] = product(side, h)
            return carry

        lax.fori_loop(0, 2, give, 0)
        start(part_copy(c, d))
        lax.fori_loop(0, 2, keep, 0)

    def activate(u):
        c, d = units[u]
        off, width = up_cuts[c]
        level = zbit if d == 0 else 1 - zbit
        part_copy(c, d).wait_recv()

        def body(p, carry):
            where = pl.ds(pl.multiple_of(p * own, 16), own)
            total = part_keep[u % 2, where, :width] + part_in[d, where, off : off + width].astype(F32)
            hidden[side, p, level, :, off : off + width] = jax.nn.gelu(
                total, approximate=True).astype(BF16)
            return carry

        lax.fori_loop(0, n_tensor, body, 0)
        start(act_copy(c, d, side))

    arrived = set()
    last_cut = len(up_cuts) - 1
    units = [(c, d) for c in range(max(last_cut - 1, 0)) for d in range(2)]
    units += [(c, d) for d in range(2) for c in range(max(last_cut - 1, 0), last_cut + 1)]
    steps = [(e, s, b) for e in range(3) for s in range(bits + 1) for b in range(subs)]
    steps.sort(key=lambda item: ((item[0] * subs + item[2]) + 2 * item[1], item[1]))
    steps.sort(key=lambda item: item[0] > 0)
    first_ready = max(n for n, item in enumerate(steps) if item[0] == 0)
    for n, item in enumerate(steps):
        advance(*item)
        if n == first_ready:
            first_product(0)
        if item == (1, 0, subs - 1):
            for c in range(1, len(up_cuts)):
                send_ups(c)
            for m, c in groups[:early]:
                send_downs(m, c)
    for u in range(1, len(units)):
        first_product(u)
        activate(u - 1)
    for m, c in groups[early:]:
        send_downs(m, c)

    order = [(2 * m + p, c) for m, c in groups for p in range(2)]
    near_count = 2 * len(down_cuts)
    items = [(t, d) for d in range(2) for t in range(near_count)]
    items += [(t, d) for t in range(near_count, len(order)) for d in range(2)]
    base = place - zbit

    def slab_of(p):
        return flip(base, p - p % 2) + p % 2

    def level_copy(level, q):
        width = down_cuts[order[items[q][0]][1]][1]
        return remote(gives[level].at[q % GIVE_RING, :, :, :width],
                      takes[level].at[q % TAKE_RING, :, :, :width],
                      red_s.at[level, q], red_r.at[level, q], device(0, 1 << level))

    def pair_copy(n):
        width = down_cuts[order[n][1]][1]
        return remote(pair_give.at[n % GIVE_RING, :, :, :width],
                      pair_take.at[n % TAKE_RING, :, :, :width],
                      pair_s.at[n], pair_r.at[n], device(2))

    def far_copy(t):
        p, c = order[t]
        off, width = down_cuts[c]
        return remote(last_give.at[t % GIVE_RING, :, :width],
                      far_in.at[slab_of(p), :, off : off + width],
                      far_s.at[t], far_r.at[t], device(1))

    def second_product(q):
        t, d = items[q]
        p, c = order[t]
        off, width = down_cuts[c]
        slab = slab_of(p)
        level = zbit if d == 0 else 1 - zbit
        if t not in landed:
            landed.add(t)
            block = down_all.at[slab, :, off : off + width]
            pltpu.make_async_copy(block, block, down_r.at[c, p + zbit * (1 - 2 * (p % 2))]).wait()
        if q >= GIVE_RING:
            level_copy(0, q - GIVE_RING).wait_send()

        def product(part):
            left = hidden[:, pl.ds(part * hp, hp), level].reshape(2 * hp * own, half)
            out = jnp.dot(left, down_all[slab, :, off : off + width], preferred_element_type=F32)
            return out.astype(BF16).reshape(2, hp * own, width)

        gives[0][q % GIVE_RING, :, :, :width] = product(1 - core)
        level_copy(0, q).start()
        keeps[0][q % 2, :, :, :width] = product(core)

    def reduce_level(level, q):
        t, d = items[q]
        p, c = order[t]
        off, width = down_cuts[c]
        slab = slab_of(p)
        level_copy(level, q).wait_recv()
        extent = extents[level]

        def total(x, first, count):
            taken = takes[level][q % TAKE_RING, x, pl.ds(first, count), :width].astype(F32)
            return keeps[level][q % 2, x, pl.ds(first, count), :width].astype(F32) + taken

        if level < bits - 1:
            if q >= GIVE_RING:
                level_copy(level + 1, q - GIVE_RING).wait_send()
            count = extent // 2
            bit = bit_of(col, level + 1)
            away = pl.multiple_of((1 - bit) * count, 16)
            here = pl.multiple_of(bit * count, 16)
            for x in range(2):
                gives[level + 1][q % GIVE_RING, x, :, :width] = total(x, away, count).astype(BF16)
            level_copy(level + 1, q).start()
            for x in range(2):
                keeps[level + 1][q % 2, x, :, :width] = total(x, here, count)
        elif d == 0:
            mine = 2 * slab + side
            stream[mine, :, off : off + width] += (
                mod_all[mine, 2:3, off : off + width] * total(side, 0, extent))
            far_keep[slab, :, off : off + width] = total(other, 0, extent)
        else:
            if t >= GIVE_RING:
                pair_copy(t - GIVE_RING).wait_send()
            for x in range(2):
                pair_give[t % GIVE_RING, x, :, :width] = total(x, 0, extent).astype(BF16)
            pair_copy(t).start()

    def join_pair(q):
        t, d = items[q]
        if d == 0:
            return
        p, c = order[t]
        off, width = down_cuts[c]
        slab = slab_of(p)
        pair_copy(t).wait_recv()
        if t >= GIVE_RING:
            far_copy(t - GIVE_RING).wait_send()
        last_give[t % GIVE_RING, :, :width] = (
            far_keep[slab, :, off : off + width]
            + pair_take[t % TAKE_RING, other, :, :width].astype(F32)).astype(BF16)
        far_copy(t).start()
        mine = 2 * slab + side
        stream[mine, :, off : off + width] += (
            mod_all[mine, 2:3, off : off + width]
            * pair_take[t % TAKE_RING, side, :, :width].astype(F32))

    landed = set()
    count = len(items)
    for i in range(count + bits + 1):
        if i == 0:
            for c, d in units:
                if d == 0:
                    act_copy(c, d, other).wait_recv()
        if i == ACT_AT:
            activate(len(units) - 1)
        if i == near_count:
            for c, d in units:
                if d == 1:
                    act_copy(c, d, other).wait_recv()
        if i < count:
            second_product(i)
        for level in range(bits):
            q = i - 1 - level
            if 0 <= q < count:
                reduce_level(level, q)
        if 0 <= i - 1 - bits < count:
            join_pair(i - 1 - bits)

    for copy in pending:
        copy.wait_send()
    for q in range(max(count - GIVE_RING, 0), count):
        for level in range(bits):
            level_copy(level, q).wait_send()
    for t in range(max(len(order) - GIVE_RING, 0), len(order)):
        pair_copy(t).wait_send()
        far_copy(t).wait_send()
    for t in range(len(order)):
        far_copy(t).wait_recv()

    def finish(r, carry):
        where = pl.ds(pl.multiple_of(r * tile, tile), tile)
        for k in range(line):
            theirs = 2 * k + other
            stream[theirs, where, :] += mod_all[theirs, 2:3, :] * far_in[k, where, :].astype(F32)
        centred, scale = moments([stream[s, where, :] for s in range(n_tm)])
        for s in range(n_tm):
            normed[s % 2, where, (s // 2) * depth : (s // 2 + 1) * depth] = (
                centred[s] * scale).astype(BF16)
        return carry

    lax.fori_loop(0, own // tile, finish, 0)
    drift = None
    for s in range(n_tm):
        part = jnp.dot(normed[s % 2, :, (s // 2) * depth : (s // 2 + 1) * depth],
                       head[s * depth : (s + 1) * depth, :], preferred_element_type=F32)
        drift = part if drift is None else drift + part
    drift_out[...] = drift

    first = jnp.where(me == 0, 1.0, 0.0)
    term = first * latents[...] - sizes[0] * drift
    short = own // 2
    packed = jnp.concatenate([term[:short], term[short:]], axis=1)
    terms[0] = packed
    beside = remote(terms.at[0], terms.at[1], sum_s.at[0], sum_r.at[0], device(1))
    beside.start()
    beside.wait()
    couples[place] = terms[0] + terms[1]
    sums = []
    for k in range(1, line):
        copy = remote(couples.at[place], couples.at[place], sum_s.at[k], sum_r.at[k], device(2 * k))
        copy.start()
        sums.append(copy)
    total = terms[0] + jnp.where(side == 1, 1.0, 0.0) * terms[1]
    for k in range(1, line):
        source = flip(place, k)
        block = couples.at[source]
        remote(block, block, sum_s.at[k], sum_r.at[k], device(2 * k)).wait_recv()
        total = total + jnp.where(source < place, 1.0, 0.0) * couples[source]
    channels = latents.shape[1]
    new_out[:short, :] = total[:, :channels]
    new_out[short:, :] = total[:, channels:]
    for copy in sums:
        copy.wait_send()


def run_block(latent, stream, feature, sizes, embed, mods, ups, downs, head, n_tm, n_tensor,
              true_depth):
    line, bits = n_tm // 2, n_tensor.bit_length() - 1
    levels = bits
    own, channels = latent.shape
    depth, half = ups.shape[0], downs.shape[0] // 2
    rows = n_tensor * own
    subs = 2 if own % 32 == 0 else 1
    up_n, down_n = len(cut(half)), len(cut(depth))
    chunks = down_n * line
    wide = min(256, depth)
    extents = [rows // 2 >> b for b in range(levels)]
    vmem, dma = pltpu.VMEM, pltpu.SemaphoreType.DMA
    scratch = [
        vmem((2, n_tensor, 2, own, line * depth), BF16),
        vmem((line, depth, half), BF16),
        vmem((line, half, depth), BF16),
        vmem((2, rows, half), BF16),
        vmem((2, rows, half), BF16),
        vmem((2, rows, min(256, half)), F32),
        vmem((2, n_tensor, 2, own, half), BF16),
        vmem((line, own, depth), BF16),
        vmem((GIVE_RING, own, wide), BF16),
        vmem((2, own, n_tm * depth), BF16),
        vmem((n_tensor, own, channels), BF16),
        vmem(mods.shape, BF16),
        vmem((n_tm, 8, depth), F32),
        vmem((n_tm, own, depth), F32),
        vmem((2, own, line * depth), BF16),
        vmem((2, own // 2, 2 * channels), F32),
        vmem((line, own // 2, 2 * channels), F32),
        vmem((line, own, depth), F32),
        vmem((GIVE_RING, 2, own, wide), BF16),
        vmem((TAKE_RING, 2, own, wide), BF16),
    ]
    scratch += [vmem((GIVE_RING, 2, extent, wide), BF16) for extent in extents]
    scratch += [vmem((TAKE_RING, 2, extent, wide), BF16) for extent in extents]
    scratch += [
        vmem((2, 2, extent, wide), BF16 if level == 0 else F32)
        for level, extent in enumerate(extents)
    ]
    scratch += [
        dma((n_tensor,)), dma(()), dma((n_tensor,)), dma((n_tensor,)), dma((n_tensor,)),
        dma((n_tensor,)), dma((3, subs)), dma((3, subs)), dma((3, bits, subs)),
        dma((3, bits, subs)), dma((up_n, line)), dma((up_n, line)), dma((down_n, line)),
        dma((down_n, line)), dma((up_n, 2)), dma((up_n, 2)), dma((up_n, 2)), dma((up_n, 2)),
        dma((levels, 2 * chunks)), dma((levels, 2 * chunks)), dma((chunks,)), dma((chunks,)),
        dma((chunks,)), dma((chunks,)),
        dma((line,)), dma((line,)),
    ]
    any_spec = pl.BlockSpec(memory_space=pl.ANY)
    vmem_spec = pl.BlockSpec(memory_space=pltpu.VMEM)
    smem_spec = pl.BlockSpec(memory_space=pltpu.SMEM)
    return pl.pallas_call(
        functools.partial(
            block_kernel, (n_tm, n_tensor, own, true_depth, depth, half, subs)),
        out_shape=(jax.ShapeDtypeStruct((own, channels), F32),) * 2,
        in_specs=[vmem_spec, any_spec, vmem_spec, smem_spec, vmem_spec, any_spec, any_spec,
                  any_spec, vmem_spec],
        out_specs=(vmem_spec,) * 2,
        scratch_shapes=scratch,
        compiler_params=pltpu.CompilerParams(
            collective_id=0, has_side_effects=True, vmem_limit_bytes=67043328
        ),
    )(latent, stream, feature, sizes, embed, mods, ups, downs, head)


def make_local(n_tm, n_tensor):
    def local(
        latents,
        residual,
        timesteps,
        step_sizes,
        embed_weight,
        mod_weight,
        up_weight,
        down_weight,
        head_weight,
    ):
        depth = up_weight.shape[0]
        half = up_weight.shape[1] // 2
        pad_d, pad_h = -depth % LANE, -half % LANE

        def widen(values, axis, parts, extra):
            if not extra:
                return values
            shape = values.shape
            split = values.reshape(shape[:axis] + (parts, -1) + shape[axis + 1 :])
            pads = [(0, 0)] * split.ndim
            pads[axis + 1] = (0, extra)
            return jnp.pad(split, pads).reshape(shape[:axis] + (-1,) + shape[axis + 1 :])

        feature = jax.nn.silu(time_features(timesteps, mod_weight.shape[1])).astype(BF16)
        drift, new_latent = run_block(
            latents[0],
            widen(residual[0], 1, n_tm, pad_d),
            feature,
            step_sizes,
            widen(embed_weight, 1, n_tm, pad_d),
            widen(mod_weight, 2, n_tm // n_tensor, pad_d),
            widen(widen(up_weight, 1, 2, pad_h), 0, 1, pad_d),
            widen(widen(down_weight, 0, 2, pad_h), 1, 1, pad_d),
            widen(head_weight, 0, n_tm, pad_d),
            n_tm,
            n_tensor,
            depth,
        )
        return (drift[None], new_latent[None])

    return local


def solution(mesh):
    in_specs = (
        P("tm", "tensor", None),
        P("tm", None, None),
        P("tm"),
        P("tm"),
        P(),
        P(None, None, "tensor"),
        P("tm", "tensor"),
        P("tensor", "tm"),
        P(),
    )
    out_specs = (P("tm", "tensor", None), P("tm", "tensor", None))
    local = make_local(mesh.shape["tm"], mesh.shape["tensor"])
    return jax.shard_map(local, mesh=mesh, in_specs=in_specs, out_specs=out_specs, check_vma=False)
```

time: 362 us -> 307 us (0.85)
  other arithmetic: 27.7 us -> 0.64 us
  Pallas kernels: 284 us -> 297 us
  blocking collectives: 12.9 us -> 0 us
  matrix products: 11.4 us -> 0 us
  starting transfers between devices: 10.8 us -> 0 us
  waiting for transfers between devices: 4.11 us -> 0 us
    all_gather x2 -> x0, blocking collectives: 12.9 us -> none  [the longest x1 7.61 us: local(): every_latent = lax.all_gather(latent_bf, 'tensor', axis=0, tiled=True)]
    pallas_call x1, Pallas kernels: 284 us -> 297 us  [run_block(): pl.pallas_call(functools.partial(block_kernel, (n_tm, n_tensor, own, true...]
    convert_element_type x4 -> x1, other arithmetic: 12.7 us -> 0.59 us  [local(): jax.nn.silu(time_features(timesteps, mod_weight.shape[1])).astype(BF16)]
    dot_general x4 -> x0, matrix products: 11.4 us -> none  [the longest x1 5.06 us: local(): jnp.dot(every_latent, embed_weight, preferred_element_type=F32)]
    ppermute x4 -> x0, starting transfers between devices: 10.8 us -> none  [the longest x3 8.62 us: local(): new_latent = new_latent + lax.ppermute(couple, 'tm', ahead)]
    unnamed x7 -> x0, other arithmetic: 6.8 us -> none
    ppermute x4 -> x0, waiting for transfers between devices: 4.11 us -> none  [the longest x1 2.24 us: local(): beside = lax.ppermute(term, 'tm', swap)]
    another operation x3 -> x0, other arithmetic: 4.08 us -> none  [local(): normed = jnp.stack(sides)]
  transfers between devices with their start and end apart: 4 -> 0, of which waited for: 3 -> 0; matrix products, arithmetic and copies ran while one was open for 0% -> 0% of each run, Pallas kernels for 0% -> 0%
where the time goes in v1:
time: 307 us
  Pallas kernels  297 us (97%)
  local copies, waits for them, and re-layouts  7.1 us (2%)
    pallas_call x1, Pallas kernels, run_block(): pl.pallas_call(functools.partial(block_kernel, (n_tm, n_tensor, own, true...  297 us
    unnamed x4, local copies, waits for them, and re-layouts  7.1 us

profile of v1, /device:TPU:0, one launch (start us, length us, event | category | flops | bytes accessed | tf_op | source)
XLA Modules:
  0.0 306.7 jit_solution(7609106430648750979)
XLA Ops:
  2.0 0.6 fusion.features
  2.6 1.6 copy.11
  4.1 2.3 copy.12.head
  6.5 297.0 %shard_map.104 = (f32[160,64]{1,0:T(8,128)}, f32[160,64]{1,0:T(8,128)}) custom-call(f32[160,64]{1,0:T(8,128)} %bitcast.10, bf16[640,5120]{1,0:T(8,128)(2,1)} %bitcast.9, bf16[1,256]{1,0:T(2,128)(2,1)} %fusion.features, f32[1]{0:T(128)S(6)} %copy.16.sizes, bf16[64,5120]{1,0:T(8,128)(2,1)} %embed.1, bf16[3,256,1280]{2,1,0:T(8,128)(2,1)} %mods.1, ...), custom_call_target="tpu_custom_call" | custom-call | tf_op jit(solution)/shard_map/pallas_call | solution.py:602
  303.5 1.6 copy.13
  305.1 1.6 copy.14
  (1 shorter events, 0.0 us)

commit v2 on v1

--- a/solution.py
+++ b/solution.py
@@ -12,9 +12,10 @@
 F32 = jnp.float32
 BF16 = jnp.bfloat16
 LANE = 128
-GIVE_RING = 3
-TAKE_RING = 4
-ACT_AT = 2
+GIVE_RING = 4
+KEEP_RING = 3
+TAKE_RING = 6
+LAG = 2
 
 
 def time_features(stamps, width):
@@ -61,13 +62,13 @@
     up_cuts, down_cuts = cut(half), cut(depth)
     (acts, up_all, down_all, part_out, part_in, part_keep, hidden, far_in, last_give,
      rows_in, lat_all, mod_in, mod_all, stream, normed, terms, couples,
-     far_keep, pair_give, pair_take) = scratch[:20]
-    gives = scratch[20 : 20 + levels]
-    takes = scratch[20 + levels : 20 + 2 * levels]
-    keeps = scratch[20 + 2 * levels : 20 + 3 * levels]
+     far_keep, pair_give, pair_take, stats) = scratch[:21]
+    gives = scratch[21 : 21 + levels]
+    takes = scratch[21 + levels : 21 + 2 * levels]
+    keeps = scratch[21 + 2 * levels : 21 + 3 * levels]
     (row_sem, mod_sem, lat_s, lat_r, modu_s, modu_r, swap_s, swap_r, spread_s, spread_r,
      up_s, up_r, down_s, down_r, part_s, part_r, act_s, act_r, red_s, red_r, pair_s, pair_r,
-     far_s, far_r, sum_s, sum_r) = scratch[20 + 3 * levels :]
+     far_s, far_r, sum_s, sum_r) = scratch[21 + 3 * levels :]
 
     me, col = lax.axis_index("tm"), lax.axis_index("tensor")
     place, side = lax.div(me, jnp.int32(2)), lax.rem(me, jnp.int32(2))
@@ -109,7 +110,7 @@
     mod_copy.start()
     row_copy(0).start()
     row_copy(1).start()
-    lat_all[col] = latents[...].astype(BF16)
+    lat_all[col] = latents[...].T.astype(BF16)
     pl.semaphore_wait(barrier, len(peers))
 
     pending = []
@@ -175,12 +176,6 @@
         for j in range(3):
             mod_all[col * slabs + i, j : j + 1, :] = jnp.dot(
                 feature, mod_in[j, :, i * depth : (i + 1) * depth], preferred_element_type=F32)
-    for f in range(1, n_tensor):
-        start(modu_copy(f, col))
-    row_copy(0).wait()
-    for f in range(1, n_tensor):
-        modu_copy(f, flip(col, f)).wait_recv()
-
     def moments(values):
         total = values[0]
         for v in values[1:]:
@@ -194,7 +189,7 @@
         for v in centred[1:]:
             total = total + v * v
         spread = jnp.sum(total, axis=-1, keepdims=True) * (1.0 / features_total)
-        return centred, lax.rsqrt(spread + 1e-06)
+        return mean, centred, lax.rsqrt(spread + 1e-06)
 
     def hidden_slabs(slot, block, where):
         lat = lat_all[block, where, :]
@@ -205,22 +200,37 @@
                          + jnp.dot(lat, embed[:, cols], preferred_element_type=F32))
         return found
 
+    def own_stats(r, carry):
+        where = pl.ds(pl.multiple_of(r * tile, tile), tile)
+        found = hidden_slabs(0, col, where)
+        for k in range(n_tm):
+            stream[k, where, :] = found[k]
+        mean, _, scale = moments(found)
+        stats[0, where, :] = jnp.broadcast_to(mean, (tile, LANE))
+        stats[1, where, :] = jnp.broadcast_to(scale, (tile, LANE))
+        return carry
+
     def own_rows(r, carry):
         where = pl.ds(pl.multiple_of(r * tile, tile), tile)
-        found = hidden_slabs(0, col, where)
-        for s in range(n_tm):
-            stream[s, where, :] = found[s]
-        centred, scale = moments(found)
+        mean, scale = stats[0, where, :1], stats[1, where, :1]
         outs = [
-            (centred[s] * scale * (1.0 + mod_all[s, 1:2, :]) + mod_all[s, 0:1, :]).astype(BF16)
-            for s in range(n_tm)
+            ((stream[k, where, :] - mean) * scale * (1.0 + mod_all[k, 1:2, :])
+             + mod_all[k, 0:1, :]).astype(BF16)
+            for k in range(n_tm)
         ]
-        for s in range(n_tm):
-            normed[s % 2, where, (s // 2) * depth : (s // 2 + 1) * depth] = outs[s]
+        for k in range(n_tm):
+            normed[k % 2, where, (k // 2) * depth : (k // 2 + 1) * depth] = outs[k]
         for k in range(line):
             acts[side, pos, zbit, where, k * depth : (k + 1) * depth] = jnp.where(
                 side == 0, outs[2 * k], outs[2 * k + 1])
         return carry
+
+    for f in range(1, n_tensor):
+        start(modu_copy(f, col))
+    row_copy(0).wait()
+    lax.fori_loop(0, own // tile, own_stats, 0)
+    for f in range(1, n_tensor):
+        modu_copy(f, flip(col, f)).wait_recv()
 
     moves = ((1, 0), (0, 1), (1, 1))
     arrivals = [(other if dx else side, 1 - zbit if dz else zbit) for dx, dz in moves]
@@ -241,22 +251,25 @@
 
     for b in range(subs):
         lax.fori_loop(b * (chunk_rows // tile), (b + 1) * (chunk_rows // tile), own_rows, 0)
-        for e in range(3):
-            start(swap_copy(e, b))
+        start(swap_copy(0, b))
+        start(swap_copy(1, b))
+    for b in range(subs):
+        start(swap_copy(2, b))
     groups = [(m, c) for m in range(line // 2) for c in range(len(down_cuts))]
     early = len(groups) * 2 // 3
 
-    for f in range(1, n_tensor):
+    def other_rows(f, first, last):
         block = flip(col, f)
         where_pos = reversed_bits(block, bits)
-        if f + 1 < n_tensor:
-            row_copy(f + 1).start()
-        row_copy(f).wait()
-        lat_copy(f, block).wait_recv()
-
-        def other_rows(r, carry):
+        if first == 0:
+            if f + 1 < n_tensor:
+                row_copy(f + 1).start()
+            row_copy(f).wait()
+            lat_copy(f, block).wait_recv()
+
+        def body(r, carry):
             where = pl.ds(pl.multiple_of(r * tile, tile), tile)
-            centred, scale = moments(hidden_slabs(f % 2, block, where))
+            _, centred, scale = moments(hidden_slabs(f % 2, block, where))
             for k in range(line):
                 value = jnp.where(side == 0, centred[2 * k], centred[2 * k + 1])
                 value = value * scale * (1.0 + mod_all[2 * k + side, 1:2, :])
@@ -264,7 +277,7 @@
                 acts[side, where_pos, zbit, where, k * depth : (k + 1) * depth] = value.astype(BF16)
             return carry
 
-        lax.fori_loop(0, own // tile, other_rows, 0)
+        lax.fori_loop(first, last, body, 0)
 
     def spread_block(e, s, b, far_side):
         sx, sz = arrivals[e]
@@ -341,26 +354,36 @@
 
     arrived = set()
     last_cut = len(up_cuts) - 1
-    units = [(c, d) for c in range(max(last_cut - 1, 0)) for d in range(2)]
-    units += [(c, d) for d in range(2) for c in range(max(last_cut - 1, 0), last_cut + 1)]
-    steps = [(e, s, b) for e in range(3) for s in range(bits + 1) for b in range(subs)]
-    steps.sort(key=lambda item: ((item[0] * subs + item[2]) + 2 * item[1], item[1]))
-    steps.sort(key=lambda item: item[0] > 0)
-    first_ready = max(n for n, item in enumerate(steps) if item[0] == 0)
-    for n, item in enumerate(steps):
-        advance(*item)
-        if n == first_ready:
+    units = [(0, 0), (0, 1)]
+    units += [(c, d) for d in range(2) for c in range(1, last_cut + 1)]
+    agenda = []
+    for e in range(3):
+        for b in range(subs):
+            due = 6.0 + 17.5 * (e * subs + b) / subs
+            agenda.append((due, "advance", (e, 0, b)))
+            for stage in range(1, bits + 1):
+                agenda.append((due + 4.0 + 2.0 * stage, "advance", (e, stage, b)))
+    unit_due = max(item[0] for item in agenda if item[2][0] == 0) + 0.1
+    agenda.append((unit_due, "unit", None))
+    pieces = own // tile
+    for f in range(1, n_tensor):
+        middle = (pieces + 1) // 2
+        for n, part in enumerate(((0, middle), (middle, pieces))):
+            due = 4.9 + 15.0 * (2 * (f - 1) + n) / (2 * (n_tensor - 1))
+            agenda.append((due, "rows", (f,) + part))
+    agenda.sort(key=lambda item: item[0])
+    for _, kind, item in agenda:
+        if kind == "rows":
+            other_rows(*item)
+        elif kind == "unit":
             first_product(0)
-        if item == (1, 0, subs - 1):
-            for c in range(1, len(up_cuts)):
-                send_ups(c)
-            for m, c in groups[:early]:
-                send_downs(m, c)
-    for u in range(1, len(units)):
-        first_product(u)
-        activate(u - 1)
-    for m, c in groups[early:]:
-        send_downs(m, c)
+        else:
+            advance(*item)
+            if item == (1, 0, subs - 1):
+                for c in range(1, len(up_cuts)):
+                    send_ups(c)
+                for m, c in groups[:early]:
+                    send_downs(m, c)
 
     order = [(2 * m + p, c) for m, c in groups for p in range(2)]
     near_count = 2 * len(down_cuts)
@@ -410,7 +433,7 @@
 
         gives[0][q % GIVE_RING, :, :, :width] = product(1 - core)
         level_copy(0, q).start()
-        keeps[0][q % 2, :, :, :width] = product(core)
+        keeps[0][q % KEEP_RING, :, :, :width] = product(core)
 
     def reduce_level(level, q):
         t, d = items[q]
@@ -422,7 +445,7 @@
 
         def total(x, first, count):
             taken = takes[level][q % TAKE_RING, x, pl.ds(first, count), :width].astype(F32)
-            return keeps[level][q % 2, x, pl.ds(first, count), :width].astype(F32) + taken
+            return keeps[level][q % KEEP_RING, x, pl.ds(first, count), :width].astype(F32) + taken
 
         if level < bits - 1:
             if q >= GIVE_RING:
@@ -435,7 +458,7 @@
                 gives[level + 1][q % GIVE_RING, x, :, :width] = total(x, away, count).astype(BF16)
             level_copy(level + 1, q).start()
             for x in range(2):
-                keeps[level + 1][q % 2, x, :, :width] = total(x, here, count)
+                keeps[level + 1][q % KEEP_RING, x, :, :width] = total(x, here, count)
         elif d == 0:
             mine = 2 * slab + side
             stream[mine, :, off : off + width] += (
@@ -469,25 +492,52 @@
 
     landed = set()
     count = len(items)
-    for i in range(count + bits + 1):
-        if i == 0:
-            for c, d in units:
-                if d == 0:
-                    act_copy(c, d, other).wait_recv()
-        if i == ACT_AT:
-            activate(len(units) - 1)
-        if i == near_count:
-            for c, d in units:
-                if d == 1:
-                    act_copy(c, d, other).wait_recv()
+
+    def turn(i):
         if i < count:
             second_product(i)
-        for level in range(bits):
-            q = i - 1 - level
+        if 0 <= i - 1 < count:
+            reduce_level(0, i - 1)
+        for level in range(1, bits):
+            q = i - 1 - LAG * level
             if 0 <= q < count:
                 reduce_level(level, q)
-        if 0 <= i - 1 - bits < count:
-            join_pair(i - 1 - bits)
+        q = i - 1 - LAG * bits
+        if 0 <= q < count:
+            join_pair(q)
+
+    def await_acts(which):
+        for c, d in units:
+            if d == which:
+                act_copy(c, d, other).wait_recv()
+
+    turns = iter(range(count + 1 + LAG * bits))
+    half_way = 1 + last_cut
+    for u in range(1, half_way + 1):
+        first_product(u)
+        activate(u - 1)
+    for m, c in groups[early:]:
+        send_downs(m, c)
+    activate(half_way)
+    rest = list(range(half_way + 1, len(units)))
+    for u in rest[:2]:
+        first_product(u)
+    await_acts(0)
+    for n, u in enumerate(rest):
+        turn(next(turns))
+        if u > rest[0] and u + 1 < len(units):
+            first_product(u + 1)
+        turn(next(turns))
+        activate(u)
+    while True:
+        i = next(turns)
+        if i == near_count:
+            await_acts(1)
+            turn(i)
+            break
+        turn(i)
+    for i in turns:
+        turn(i)
 
     for copy in pending:
         copy.wait_send()
@@ -505,7 +555,7 @@
         for k in range(line):
             theirs = 2 * k + other
             stream[theirs, where, :] += mod_all[theirs, 2:3, :] * far_in[k, where, :].astype(F32)
-        centred, scale = moments([stream[s, where, :] for s in range(n_tm)])
+        _, centred, scale = moments([stream[s, where, :] for s in range(n_tm)])
         for s in range(n_tm):
             normed[s % 2, where, (s // 2) * depth : (s // 2 + 1) * depth] = (
                 centred[s] * scale).astype(BF16)
@@ -514,13 +564,14 @@
     lax.fori_loop(0, own // tile, finish, 0)
     drift = None
     for s in range(n_tm):
-        part = jnp.dot(normed[s % 2, :, (s // 2) * depth : (s // 2 + 1) * depth],
-                       head[s * depth : (s + 1) * depth, :], preferred_element_type=F32)
+        part = lax.dot_general(normed[s % 2, :, (s // 2) * depth : (s // 2 + 1) * depth],
+                               head[:, s * depth : (s + 1) * depth],
+                               (((1,), (1,)), ((), ())), preferred_element_type=F32)
         drift = part if drift is None else drift + part
-    drift_out[...] = drift
+    drift_out[...] = drift.T
 
     first = jnp.where(me == 0, 1.0, 0.0)
-    term = first * latents[...] - sizes[0] * drift
+    term = first * latents[...].T - sizes[0] * drift
     short = own // 2
     packed = jnp.concatenate([term[:short], term[short:]], axis=1)
     terms[0] = packed
@@ -539,9 +590,8 @@
         block = couples.at[source]
         remote(block, block, sum_s.at[k], sum_r.at[k], device(2 * k)).wait_recv()
         total = total + jnp.where(source < place, 1.0, 0.0) * couples[source]
-    channels = latents.shape[1]
-    new_out[:short, :] = total[:, :channels]
-    new_out[short:, :] = total[:, channels:]
+    channels = latents.shape[0]
+    new_out[...] = jnp.concatenate([total[:, :channels], total[:, channels:]], axis=0).T
     for copy in sums:
         copy.wait_send()
 
@@ -550,10 +600,10 @@
               true_depth):
     line, bits = n_tm // 2, n_tensor.bit_length() - 1
     levels = bits
-    own, channels = latent.shape
+    channels, own = latent.shape
     depth, half = ups.shape[0], downs.shape[0] // 2
     rows = n_tensor * own
-    subs = 2 if own % 32 == 0 else 1
+    subs = own // (32 if own % 32 == 0 else 16)
     up_n, down_n = len(cut(half)), len(cut(depth))
     chunks = down_n * line
     wide = min(256, depth)
@@ -580,11 +630,12 @@
         vmem((line, own, depth), F32),
         vmem((GIVE_RING, 2, own, wide), BF16),
         vmem((TAKE_RING, 2, own, wide), BF16),
+        vmem((2, own, LANE), F32),
     ]
     scratch += [vmem((GIVE_RING, 2, extent, wide), BF16) for extent in extents]
     scratch += [vmem((TAKE_RING, 2, extent, wide), BF16) for extent in extents]
     scratch += [
-        vmem((2, 2, extent, wide), BF16 if level == 0 else F32)
+        vmem((KEEP_RING, 2, extent, wide), BF16 if level == 0 else F32)
         for level, extent in enumerate(extents)
     ]
     scratch += [
@@ -602,7 +653,7 @@
     return pl.pallas_call(
         functools.partial(
             block_kernel, (n_tm, n_tensor, own, true_depth, depth, half, subs)),
-        out_shape=(jax.ShapeDtypeStruct((own, channels), F32),) * 2,
+        out_shape=(jax.ShapeDtypeStruct((channels, own), F32),) * 2,
         in_specs=[vmem_spec, any_spec, vmem_spec, smem_spec, vmem_spec, any_spec, any_spec,
                   any_spec, vmem_spec],
         out_specs=(vmem_spec,) * 2,
@@ -640,7 +691,7 @@
 
         feature = jax.nn.silu(time_features(timesteps, mod_weight.shape[1])).astype(BF16)
         drift, new_latent = run_block(
-            latents[0],
+            latents[0].T,
             widen(residual[0], 1, n_tm, pad_d),
             feature,
             step_sizes,
@@ -648,12 +699,12 @@
             widen(mod_weight, 2, n_tm // n_tensor, pad_d),
             widen(widen(up_weight, 1, 2, pad_h), 0, 1, pad_d),
             widen(widen(down_weight, 0, 2, pad_h), 1, 1, pad_d),
-            widen(head_weight, 0, n_tm, pad_d),
+            widen(head_weight.T, 1, n_tm, pad_d),
             n_tm,
             n_tensor,
             depth,
         )
-        return (drift[None], new_latent[None])
+        return (drift.T[None], new_latent.T[None])
 
     return local
 

time: 307 us -> 267 us (0.87)
  Pallas kernels: 297 us -> 262 us
  local copies, waits for them, and re-layouts: 7.1 us -> 2.95 us
    pallas_call x1, Pallas kernels: 297 us -> 262 us  [run_block(): pl.pallas_call(functools.partial(block_kernel, (n_tm, n_tensor, own, true...]
    unnamed x4 -> x2, local copies, waits for them, and re-layouts: 7.1 us -> 2.95 us
where the time goes in v2:
time: 267 us
  Pallas kernels  262 us (98%)
  local copies, waits for them, and re-layouts  2.95 us (1%)
    pallas_call x1, Pallas kernels, run_block(): pl.pallas_call(functools.partial(block_kernel, (n_tm, n_tensor, own, true...  262 us

profile of v2, /device:TPU:0, one launch (start us, length us, event | category | flops | bytes accessed | tf_op | source)
XLA Modules:
  0.0 267.1 jit_solution(16959811649505504111)
XLA Ops:
  2.0 0.6 fusion.features
  2.6 261.6 %shard_map.104 = (f32[64,160]{1,0:T(8,128)}, f32[64,160]{1,0:T(8,128)}) custom-call(f32[64,160]{1,0:T(8,128)} %bitcast.18, bf16[640,5120]{1,0:T(8,128)(2,1)} %bitcast.16, bf16[1,256]{1,0:T(2,128)(2,1)} %fusion.features, f32[1]{0:T(128)S(6)} %copy.14.sizes, bf16[64,5120]{1,0:T(8,128)(2,1)} %embed.1, bf16[3,256,1280]{2,1,0:T(8,128)(2,1)} %mods.1, ...), custom_call_target="tpu_custom_call" | custom-call | tf_op jit(solution)/shard_map/pallas_call | solution.py:653
  264.2 1.5 copy.15
  265.6 1.5 copy.16
  (1 shorter events, 0.0 us)

commit v3 on v2

--- a/solution.py
+++ b/solution.py
@@ -49,6 +49,12 @@
     return sum(((value >> b) & 1) << (bits - 1 - b) for b in range(bits))
 
 
+def cut_first(extent, width=256):
+    lead = extent % width
+    chunks = [(0, lead)] if lead else []
+    return chunks + [(a, width) for a in range(lead, extent, width)]
+
+
 def cut(extent, width=256):
     return [(a, min(width, extent - a)) for a in range(0, extent, width)]
 
@@ -59,7 +65,7 @@
     line, bits = n_tm // 2, n_tensor.bit_length() - 1
     levels = bits
     extents = [(n_tensor * own // 2) >> b for b in range(levels)]
-    up_cuts, down_cuts = cut(half), cut(depth)
+    up_cuts, down_cuts = cut_first(half), cut(depth)
     (acts, up_all, down_all, part_out, part_in, part_keep, hidden, far_in, last_give,
      rows_in, lat_all, mod_in, mod_all, stream, normed, terms, couples,
      far_keep, pair_give, pair_take, stats) = scratch[:21]
@@ -354,8 +360,9 @@
 
     arrived = set()
     last_cut = len(up_cuts) - 1
-    units = [(0, 0), (0, 1)]
-    units += [(c, d) for d in range(2) for c in range(1, last_cut + 1)]
+    split = max(last_cut - 1, 1)
+    units = [(c, d) for c in range(split) for d in range(2)]
+    units += [(c, d) for d in range(2) for c in range(split, last_cut + 1)]
     agenda = []
     for e in range(3):
         for b in range(subs):
@@ -512,7 +519,7 @@
                 act_copy(c, d, other).wait_recv()
 
     turns = iter(range(count + 1 + LAG * bits))
-    half_way = 1 + last_cut
+    half_way = units.index((last_cut, 0))
     for u in range(1, half_way + 1):
         first_product(u)
         activate(u - 1)

time: 267 us -> 277 us (1.037)
  Pallas kernels: 262 us -> 271 us
    pallas_call x1, Pallas kernels: 262 us -> 271 us  [run_block(): pl.pallas_call(functools.partial(block_kernel, (n_tm, n_tensor, own, true...]
where the time goes in v3:
time: 277 us; the launch traced here: 276 us
  Pallas kernels  271 us (98%)
  local copies, waits for them, and re-layouts  2.95 us (1%)
    pallas_call x1, Pallas kernels, run_block(): pl.pallas_call(functools.partial(block_kernel, (n_tm, n_tensor, own, true...  271 us

profile of v3, /device:TPU:0, one launch (start us, length us, event | category | flops | bytes accessed | tf_op | source)
XLA Modules:
  0.0 276.3 jit_solution(4845054541883715615)
XLA Ops:
  2.0 0.6 fusion.features
  2.6 270.7 %shard_map.104 = (f32[64,160]{1,0:T(8,128)}, f32[64,160]{1,0:T(8,128)}) custom-call(f32[64,160]{1,0:T(8,128)} %bitcast.18, bf16[640,5120]{1,0:T(8,128)(2,1)} %bitcast.16, bf16[1,256]{1,0:T(2,128)(2,1)} %fusion.features, f32[1]{0:T(128)S(6)} %copy.14.sizes, bf16[64,5120]{1,0:T(8,128)(2,1)} %embed.1, bf16[3,256,1280]{2,1,0:T(8,128)(2,1)} %mods.1, ...), custom_call_target="tpu_custom_call" | custom-call | tf_op jit(solution)/shard_map/pallas_call | solution.py:660
  273.3 1.5 copy.15
  274.8 1.5 copy.16
  (1 shorter events, 0.0 us)
